TPU v7x, 128 devices: a whole 4x4x4 slice. The times are simulated.
128 devices in a mesh: blk: 32 (over x, y, z_lo), segment: 4 (over z_hi, core).
Axes of the slice: x: 4, y: 4, z: 4 (z_hi: 2, z_lo: 2; z = z_hi * 2 + z_lo), core: 2. Of those that a mesh axis runs over, the one named last changes fastest.
Arguments:
- latent_queries: bfloat16 [2, 128, 2048], P(None, 'blk'), may hold values from -400 to 400
- latent_embed: bfloat16 [2, 128, 2048], P(None, 'blk'), may hold values from -6 to 6
- history_keys: bfloat16 [2, 32768, 2048], P(None, ('blk', 'segment')), may hold values from -6 to 6
- history_values: bfloat16 [2, 32768, 2048], P(None, ('blk', 'segment')), may hold values from -7 to 7
- latent_pos: int32 [2, 128], replicated, may hold values from 1 to 32768, as said below
- norm_gain: float32 [4, 2048], P('segment'), may hold values from 0.25 to 1.75
- w_qkv: bfloat16 [4, 2048, 3, 2048], P('segment', None, None, 'blk'), may hold values from -0.125 to 0.125
- w_out: bfloat16 [4, 2048, 2048], P('segment', 'blk'), may hold values from -0.125 to 0.125
Outputs:
- latents_out: float32 [2, 128, 2048], P(None, 'blk', 'segment')
Inputs may be any that keep to these rules, and one draw needn't show every extreme that they name: `latent_pos`: Non-decreasing along the latents of a micro-batch; latent i sees at least (i + 1) * 256 positions and the last latent sees all 32768.
All inputs are finite; a program needn't handle non-finite values.
Results may differ from a plain program's by a relative error of at most 0.0085.
Values may be sent and summed in bfloat16 or wider, within the bound.
A program may use at most 64 MiB of HBM per device.

v0:
```python
import jax
import jax.numpy as jnp
from jax import lax
from jax.sharding import PartitionSpec as P

HEADS = 16
epsilon = 1e-06
masked = -1e30


def from_partner(array, axis, distance):
    return lax.ppermute(array, axis, [(i, i ^ 1 << distance) for i in range(lax.axis_size(axis))])


def shifted(value, axis, steps):
    count = lax.axis_size(axis)
    first, last = (max(0, -steps), min(count, count - steps))
    return lax.ppermute(value, axis, [(source, source + steps) for source in range(first, last)])


def normalize(latent_state, gain_row):
    factor = lax.rsqrt(jnp.mean(latent_state * latent_state, axis=1, keepdims=True) + epsilon)
    return (latent_state * factor * gain_row).astype(jnp.bfloat16)


def attend_columns(mixed_qkv, head_size):
    lat_count = mixed_qkv.shape[0]
    columns = mixed_qkv.shape[1] // 3
    head_span = min(columns, head_size)
    head_groups = columns // head_span
    query_part = mixed_qkv[:, :columns].reshape(lat_count, head_groups, head_span)
    key_part = mixed_qkv[:, columns : 2 * columns].reshape(lat_count, head_groups, head_span)
    value_part = mixed_qkv[:, 2 * columns :].reshape(lat_count, head_groups, head_span)
    scores = jnp.einsum("ipd,jpd->pij", query_part, key_part, preferred_element_type=jnp.float32)
    scores = scores + from_partner(scores, "blk", 0)
    scores = scores * head_size ** (-0.5)
    row_ids = lax.broadcasted_iota(jnp.int32, (lat_count, lat_count), 0)
    col_ids = lax.broadcasted_iota(jnp.int32, (lat_count, lat_count), 1)
    scores = jnp.where((col_ids <= row_ids)[None], scores, masked)
    row_top = jnp.max(scores, axis=2, keepdims=True)
    weights = jnp.exp(scores - row_top)
    soft_weights = (weights / jnp.sum(weights, axis=2, keepdims=True)).astype(jnp.bfloat16)
    attended = jnp.einsum(
        "pij,jpd->ipd", soft_weights, value_part, preferred_element_type=jnp.float32
    )
    return attended.reshape(lat_count, columns).astype(jnp.bfloat16)


def layer_full(latent_state, gain_row, projection, output_rows, head_size):
    normed = normalize(latent_state, gain_row)
    mixed_qkv = jnp.dot(normed, projection, preferred_element_type=jnp.float32).astype(jnp.bfloat16)
    attended = attend_columns(mixed_qkv, head_size)
    update = jnp.dot(attended, output_rows, preferred_element_type=jnp.float32)
    return latent_state + lax.psum(update, "blk")


def on_device(
    latent_queries, latent_embed, history_keys, history_values, latent_pos, norm_gain, w_qkv, w_out
):
    segment_count = lax.axis_size("segment")
    blk_id = lax.axis_index("blk")
    segment_id = lax.axis_index("segment")
    micro_count = history_keys.shape[0]
    hist_rows = history_keys.shape[1]
    width = history_keys.shape[2]
    head_size = width // HEADS
    gathered = lax.all_gather(latent_queries, "blk", axis=1, tiled=True)
    lat_count = gathered.shape[1]
    first_key = (blk_id * segment_count + segment_id) * hist_rows
    key_ids = first_key + jnp.arange(hist_rows, dtype=jnp.int32)
    visible = (key_ids[None, None, :] < latent_pos[:, :, None])[:, None]
    query_heads = gathered.reshape(micro_count, lat_count, HEADS, head_size)
    key_heads = history_keys.reshape(micro_count, hist_rows, HEADS, head_size)
    value_heads = history_values.reshape(micro_count, hist_rows, HEADS, head_size)
    scores = jnp.einsum(
        "mqhd,mkhd->mhqk", query_heads, key_heads, preferred_element_type=jnp.float32
    ) * head_size ** (-0.5)
    scores = jnp.where(visible, scores, masked)
    highest = lax.pmax(jnp.max(scores, axis=3), ("blk", "segment"))
    weights = jnp.where(visible, jnp.exp(scores - highest[..., None]), 0.0)
    totals = jnp.transpose(jnp.sum(weights, axis=3), (0, 2, 1))
    partial_value = jnp.einsum(
        "mhqk,mkhd->mqhd",
        weights.astype(jnp.bfloat16),
        value_heads,
        preferred_element_type=jnp.float32,
    )
    partial_value = partial_value.reshape(micro_count, lat_count, width)
    summed, counted = (
        lax.psum_scatter(partial_value, "blk", scatter_dimension=1, tiled=True),
        lax.psum_scatter(totals, "blk", scatter_dimension=1, tiled=True),
    )
    summed, counted = lax.psum((summed, counted), "segment")
    rows_here = summed.shape[1]
    attended = (
        summed.reshape(micro_count, rows_here, HEADS, head_size) / counted[..., None]
    ).reshape(micro_count, rows_here, width)
    start_state = latent_embed.astype(jnp.float32) + attended
    gain_row = norm_gain[0]
    projection = w_qkv[0].reshape(width, -1)
    output_rows = w_out[0]
    tower_in = lax.all_gather(start_state, "blk", axis=1, tiled=True)
    rounds = micro_count + segment_count - 1
    last_segment = segment_count - 1
    incoming = jnp.zeros_like(tower_in[0])
    finished = []
    for round_index in range(rounds):
        if round_index < micro_count:
            incoming = jnp.where(segment_id == 0, tower_in[round_index], incoming)
        latent_state = layer_full(incoming, gain_row, projection, output_rows, head_size)
        if round_index >= last_segment:
            finished.append(jnp.where(segment_id == last_segment, latent_state, 0.0))
        if round_index + 1 < rounds:
            incoming = shifted(latent_state, "segment", 1)
    results = jnp.stack(finished)
    own_rows = latent_embed.shape[1]
    results = lax.dynamic_slice_in_dim(results, blk_id * own_rows, own_rows, 1)
    return lax.psum_scatter(results, "segment", scatter_dimension=2, tiled=True)


def solution(mesh):
    return jax.shard_map(
        on_device,
        mesh=mesh,
        in_specs=(
            P(None, "blk", None),
            P(None, "blk", None),
            P(None, ("blk", "segment"), None),
            P(None, ("blk", "segment"), None),
            P(),
            P("segment", None),
            P("segment", None, None, "blk"),
            P("segment", "blk", None),
        ),
        out_specs=P(None, "blk", "segment"),
        check_vma=False,
    )
```

profile of v0, /device:TPU:1, one launch (start us, length us, event | category | flops | bytes accessed | tf_op | source)
XLA Modules:
  0.0 2481.4 jit_solution(8695598158295302768)
XLA Ops:
  12.3 127.7 %all-gather.3.cloned.1.call-done = bf16[2,128,2048]{2,0,1:T(2,128)(2,1)} async-done(((bf16[2,4,2048]{2,0,1:T(2,128)(2,1)}), bf16[2,128,2048]{2,0,1:T(2,128)(2,1)}) %all-gather.3.cloned.1.call-update) | async-done | bytes 1048592 | tf_op jit(solution)/shard_map/all_gather | solution.py:67
  143.6 4.4 fusion
  148.0 87.3 %pmax.7 = f32[2,16,128]{2,1,0:T(8,128)S(1)} all-reduce(f32[2,16,128]{2,1,0:T(8,128)S(1)} %get-tuple-element.11), channel_id=1, replica_groups=mesh['blk'=32,'segment'=4] {'blk','segment'}, use_global_device_ids=true, to_apply=%region_1.2 | all-reduce | flops 4096 | bytes 32768 | tf_op jit(solution)/shard_map/pmax | solution.py:79
  235.3 5.4 fusion.3
  248.2 131.5 %all-reduce.1 = f32[2,128,16]{2,1,0:T(8,128)S(1)} all-reduce(f32[2,128,16]{2,1,0:T(8,128)S(1)} %copy.23), channel_id=3, replica_groups=mesh['blk'=32,'segment'=4] {'blk'}, use_global_device_ids=true, to_apply=%region_5.6.clone | all-reduce | flops 4096 | bytes 32768
  379.8 153.2 %all-reduce.22.cloned.1.call-done = f32[2,128,2048]{2,1,0:T(8,128)} async-done(((f32[2,128,2048]{2,1,0:T(8,128)}), f32[2,128,2048]{2,1,0:T(8,128)}) %all-reduce.22.cloned.1.call-update) | async-done | bytes 2097168
  534.6 29.4 %psum.50 = f32[2,4,16]{2,1,0:T(4,128)S(1)} all-reduce(f32[2,4,16]{2,1,0:T(4,128)S(1)} %constant_dynamic-slice_fusion), channel_id=1, replica_groups=mesh['blk'=32,'segment'=4] {'segment'}, use_global_device_ids=true, to_apply=%region_6.7 | all-reduce | flops 128 | bytes 1024 | tf_op jit(solution)/shard_map/psum | solution.py:93
  564.2 34.6 %all-reduce.10.cloned.1.call-done = f32[2,4,2048]{2,1,0:T(4,128)} async-done(((f32[2,4,2048]{2,1,0:T(4,128)}), f32[2,4,2048]{2,1,0:T(4,128)}) %all-reduce.10.cloned.1.call-update) | async-done | bytes 65552 | tf_op jit(solution)/shard_map/psum | solution.py:93
  600.4 128.9 %all-gather.5.cloned.1.call-done = f32[2,128,2048]{2,0,1:T(2,128)} async-done(((f32[2,4,2048]{2,0,1:T(2,128)}), f32[2,128,2048]{2,0,1:T(2,128)}) %all-gather.5.cloned.1.call-update) | async-done | bytes 2097168 | tf_op jit(solution)/shard_map/all_gather | solution.py:102
  729.2 5.4 fusion.100
  741.7 311.0 %all-reduce.12.cloned.1.call-done = f32[128,2048]{1,0:T(8,128)} async-done(((f32[128,2048]{1,0:T(8,128)}), f32[128,2048]{1,0:T(8,128)}) %all-reduce.12.cloned.1.call-update) | async-done | bytes 1048592 | tf_op jit(solution)/shard_map/psum | solution.py:54
  1054.8 28.3 %collective-permute-start.1 = (f32[128,2048]{1,0:T(8,128)S(1)}, f32[128,2048]{1,0:T(8,128)S(1)}, u32[]{:S(2)}, u32[]{:S(2)}) collective-permute-start(f32[128,2048]{1,0:T(8,128)S(1)} %bitcast_add_fusion), channel_id=1, source_target_pairs={{0,1},{1,2},{2,3},{4,5},{5,6},{6,7},{8,9},{9,10},{10,11},{12,13},{... | collective-permute-start | bytes 3145736 | tf_op jit(solution)/shard_map/ppermute | solution.py:18
  1083.1 12.2 collective-permute-done.1
  1103.7 289.7 %all-reduce.14.cloned.1.call-done = f32[128,2048]{1,0:T(8,128)} async-done(((f32[128,2048]{1,0:T(8,128)}), f32[128,2048]{1,0:T(8,128)}) %all-reduce.14.cloned.1.call-update) | async-done | bytes 1048592 | tf_op jit(solution)/shard_map/psum | solution.py:54
  1395.1 28.1 %collective-permute-start.3 = (f32[128,2048]{1,0:T(8,128)S(1)}, f32[128,2048]{1,0:T(8,128)S(1)}, u32[]{:S(2)}, u32[]{:S(2)}) collective-permute-start(f32[128,2048]{1,0:T(8,128)S(1)} %add.118), channel_id=1, source_target_pairs={{0,1},{1,2},{2,3},{4,5},{5,6},{6,7},{8,9},{9,10},{10,11},{12,13},{... | collective-permute-start | bytes 3145736 | tf_op jit(solution)/shard_map/ppermute | solution.py:18
  1423.2 12.4 collective-permute-done.3
  1442.1 289.7 %all-reduce.16.cloned.1.call-done = f32[128,2048]{1,0:T(8,128)} async-done(((f32[128,2048]{1,0:T(8,128)}), f32[128,2048]{1,0:T(8,128)}) %all-reduce.16.cloned.1.call-update) | async-done | bytes 1048592 | tf_op jit(solution)/shard_map/psum | solution.py:54
  1733.5 28.1 %collective-permute-start.5 = (f32[128,2048]{1,0:T(8,128)S(1)}, f32[128,2048]{1,0:T(8,128)S(1)}, u32[]{:S(2)}, u32[]{:S(2)}) collective-permute-start(f32[128,2048]{1,0:T(8,128)S(1)} %add.121), channel_id=1, source_target_pairs={{0,1},{1,2},{2,3},{4,5},{5,6},{6,7},{8,9},{9,10},{10,11},{12,13},{... | collective-permute-start | bytes 3145736 | tf_op jit(solution)/shard_map/ppermute | solution.py:18
  1761.6 12.4 collective-permute-done.5
  1780.6 289.6 %all-reduce.18.cloned.1.call-done = f32[128,2048]{1,0:T(8,128)} async-done(((f32[128,2048]{1,0:T(8,128)}), f32[128,2048]{1,0:T(8,128)}) %all-reduce.18.cloned.1.call-update) | async-done | bytes 1048592 | tf_op jit(solution)/shard_map/psum | solution.py:54
  2072.9 28.1 %collective-permute-start.7 = (f32[128,2048]{1,0:T(8,128)S(1)}, f32[128,2048]{1,0:T(8,128)S(1)}, u32[]{:S(2)}, u32[]{:S(2)}) collective-permute-start(f32[128,2048]{1,0:T(8,128)S(1)} %get-tuple-element.6), channel_id=1, source_target_pairs={{0,1},{1,2},{2,3},{4,5},{5,6},{6,7},{8,9},{9,10},{10,11},{12,13},{... | collective-permute-start | bytes 3145736 | tf_op jit(solution)/shard_map/ppermute | solution.py:18
  2101.0 12.4 collective-permute-done.7
  2119.5 289.7 %all-reduce.20.cloned.1.call-done = f32[128,2048]{1,0:T(8,128)} async-done(((f32[128,2048]{1,0:T(8,128)}), f32[128,2048]{1,0:T(8,128)}) %all-reduce.20.cloned.1.call-update) | async-done | bytes 1048592 | tf_op jit(solution)/shard_map/psum | solution.py:54
  2417.4 55.1 %reduce-scatter.6.cloned.1.call-done = f32[512,8]{1,0:T(8,128)} async-done(((f32[2048,8]{1,0:T(8,128)}), f32[512,8]{1,0:T(8,128)}) %reduce-scatter.6.cloned.1.call-update) | async-done | bytes 16400
  (114 shorter events, 72.2 us)
Async XLA Ops:
  6.5 137.1 %copy-start = (bf16[2,256,2048]{2,1,0:T(8,128)(2,1)S(1)}, bf16[2,256,2048]{2,1,0:T(8,128)(2,1)}, u32[]{:S(2)}) copy-start(bf16[2,256,2048]{2,1,0:T(8,128)(2,1)} %param.10) | copy-start | bytes 6291460
  6.5 133.4 %all-gather.3.cloned.1.call-start = ((), (), s32[]{:S(2)}) async-start(), calls=%async_computation.1 | async-start | bytes 1081344 | tf_op jit(solution)/shard_map/all_gather | solution.py:67
  8.1 524.9 %all-reduce.22.cloned.1.call-start = ((), (), s32[]{:S(2)}) async-start(), calls=%async_computation.10 | async-start | bytes 4194304
  243.6 355.1 %copy-start.9 = (bf16[2,4,2048]{2,1,0:T(4,128)(2,1)S(1)}, bf16[2,4,2048]{2,1,0:T(4,128)(2,1)}, u32[]{:S(2)}) copy-start(bf16[2,4,2048]{2,1,0:T(4,128)(2,1)} %param.9) | copy-start | bytes 98308
  243.7 355.1 %all-reduce.10.cloned.1.call-start = ((), (), s32[]{:S(2)}) async-start(), calls=%async_computation.2 | async-start | bytes 131072 | tf_op jit(solution)/shard_map/psum | solution.py:93
  248.1 487.5 %copy-start.1 = (bf16[1,2048,3,64]{1,3,2,0:T(8,128)(2,1)S(1)}, bf16[1,2048,3,64]{1,3,2,0:T(8,128)(2,1)}, u32[]{:S(2)}) copy-start(bf16[1,2048,3,64]{1,3,2,0:T(8,128)(2,1)} %param.14) | copy-start | bytes 2359300
  248.1 487.5 %copy-start.8 = (f32[1,2048]{1,0:T(1,128)S(1)}, f32[1,2048]{1,0:T(1,128)}, u32[]{:S(2)}) copy-start(f32[1,2048]{1,0:T(1,128)} %param.13) | copy-start | bytes 24580
  534.6 205.6 %copy-start.7 = (bf16[1,64,2048]{2,1,0:T(8,128)(2,1)S(1)}, bf16[1,64,2048]{2,1,0:T(8,128)(2,1)}, u32[]{:S(2)}) copy-start(bf16[1,64,2048]{2,1,0:T(8,128)(2,1)} %param.15) | copy-start | bytes 786436
  534.6 194.7 %all-gather.5.cloned.1.call-start = ((), (), s32[]{:S(2)}) async-start(), calls=%async_computation.3 | async-start | bytes 2162688 | tf_op jit(solution)/shard_map/all_gather | solution.py:102
  600.3 452.5 %all-reduce.12.cloned.1.call-start = ((), (), s32[]{:S(2)}) async-start(), calls=%async_computation.4 | async-start | bytes 2097152 | tf_op jit(solution)/shard_map/psum | solution.py:54
  736.4 3.7 collective-permute-start
  741.7 651.7 %all-reduce.14.cloned.1.call-start = ((), (), s32[]{:S(2)}) async-start(), calls=%async_computation.5 | async-start | bytes 2097152 | tf_op jit(solution)/shard_map/psum | solution.py:54
  1054.8 40.6 %collective-permute-start.1 = (f32[128,2048]{1,0:T(8,128)S(1)}, f32[128,2048]{1,0:T(8,128)S(1)}, u32[]{:S(2)}, u32[]{:S(2)}) collective-permute-start(f32[128,2048]{1,0:T(8,128)S(1)} %bitcast_add_fusion), channel_id=1, source_target_pairs={{0,1},{1,2},{2,3},{4,5},{5,6},{6,7},{8,9},{9,10},{10,11},{12,13},{... | collective-permute-start | bytes 3145736 | tf_op jit(solution)/shard_map/ppermute | solution.py:18
  1098.9 3.2 collective-permute-start.2
  1103.7 628.1 %all-reduce.16.cloned.1.call-start = ((), (), s32[]{:S(2)}) async-start(), calls=%async_computation.6 | async-start | bytes 2097152 | tf_op jit(solution)/shard_map/psum | solution.py:54
  1395.1 40.6 %collective-permute-start.3 = (f32[128,2048]{1,0:T(8,128)S(1)}, f32[128,2048]{1,0:T(8,128)S(1)}, u32[]{:S(2)}, u32[]{:S(2)}) collective-permute-start(f32[128,2048]{1,0:T(8,128)S(1)} %add.118), channel_id=1, source_target_pairs={{0,1},{1,2},{2,3},{4,5},{5,6},{6,7},{8,9},{9,10},{10,11},{12,13},{... | collective-permute-start | bytes 3145736 | tf_op jit(solution)/shard_map/ppermute | solution.py:18
  1437.3 3.2 collective-permute-start.4
  1442.1 628.1 %all-reduce.18.cloned.1.call-start = ((), (), s32[]{:S(2)}) async-start(), calls=%async_computation.7 | async-start | bytes 2097152 | tf_op jit(solution)/shard_map/psum | solution.py:54
  1733.5 40.6 %collective-permute-start.5 = (f32[128,2048]{1,0:T(8,128)S(1)}, f32[128,2048]{1,0:T(8,128)S(1)}, u32[]{:S(2)}, u32[]{:S(2)}) collective-permute-start(f32[128,2048]{1,0:T(8,128)S(1)} %add.121), channel_id=1, source_target_pairs={{0,1},{1,2},{2,3},{4,5},{5,6},{6,7},{8,9},{9,10},{10,11},{12,13},{... | collective-permute-start | bytes 3145736 | tf_op jit(solution)/shard_map/ppermute | solution.py:18
  1775.7 3.2 collective-permute-start.6
  1780.5 628.7 %all-reduce.20.cloned.1.call-start = ((), (), s32[]{:S(2)}) async-start(), calls=%async_computation.8 | async-start | bytes 2097152 | tf_op jit(solution)/shard_map/psum | solution.py:54
  2072.9 40.5 %collective-permute-start.7 = (f32[128,2048]{1,0:T(8,128)S(1)}, f32[128,2048]{1,0:T(8,128)S(1)}, u32[]{:S(2)}, u32[]{:S(2)}) collective-permute-start(f32[128,2048]{1,0:T(8,128)S(1)} %get-tuple-element.6), channel_id=1, source_target_pairs={{0,1},{1,2},{2,3},{4,5},{5,6},{6,7},{8,9},{9,10},{10,11},{12,13},{... | collective-permute-start | bytes 3145736 | tf_op jit(solution)/shard_map/ppermute | solution.py:18
  2114.7 3.2 collective-permute-start.8
  2119.4 353.1 %reduce-scatter.6.cloned.1.call-start = ((), (), s32[]{:S(2)}) async-start(), calls=%async_computation.9 | async-start | bytes 1310720
  (7 other events, 13.6 us)
Sparse Core Ops, SparseCore 0:
  9.0 130.9 all-gather.2
  243.8 289.1 all-reduce.21
  535.5 63.2 all-reduce.9
  600.4 128.7 all-gather.4
  741.8 310.9 all-reduce.11
  1103.8 289.5 all-reduce.13
  1442.2 289.5 all-reduce.15
  1780.6 289.4 all-reduce.17
  2119.5 289.6 all-reduce.19
  2417.5 54.9 reduce-scatter.5
where the time goes:
time: 2480 us
  waiting for transfers between devices  2030 us (82%)
  blocking collectives  248 us (10%)
  starting transfers between devices  116 us (5%)
  local copies, waits for them, and re-layouts  31.8 us (1%)
    psum x5, waiting for transfers between devices, layer_full(): return latent_state + lax.psum(update, 'blk')  1470 us
    unnamed x12, waiting for transfers between devices  208 us
    unnamed x1, blocking collectives  132 us
    all_gather x1, waiting for transfers between devices, on_device(): tower_in = lax.all_gather(start_state, 'blk', axis=1, tiled=True)  129 us
    all_gather x1, waiting for transfers between devices, on_device(): gathered = lax.all_gather(latent_queries, 'blk', axis=1, tiled=True)  128 us
    ppermute x4, starting transfers between devices, shifted(): lax.ppermute(value, axis, [(source, source + steps) for source in range(f...  113 us
    pmax x1, blocking collectives, on_device(): highest = lax.pmax(jnp.max(scores, axis=3), ('blk', 'segment'))  87.3 us
  transfers between devices with their start and end apart: 19, of which 19 were waited for; matrix products, arithmetic and copies ran while one was open for 0% of the time, Pallas kernels for 0%

commit v1 on v0

--- a/solution.py
+++ b/solution.py
@@ -51,7 +51,7 @@
     mixed_qkv = jnp.dot(normed, projection, preferred_element_type=jnp.float32).astype(jnp.bfloat16)
     attended = attend_columns(mixed_qkv, head_size)
     update = jnp.dot(attended, output_rows, preferred_element_type=jnp.float32)
-    return latent_state + lax.psum(update, "blk")
+    return latent_state + jnp.sum(lax.all_gather(update, "blk"), axis=0)
 
 
 def on_device(

time: 2480 us -> 4530 us (1.83)
  waiting for transfers between devices: 2030 us -> 4130 us
  starting transfers between devices: 116 us -> 23 us
  other arithmetic: 17.9 us -> 70.1 us
    all_gather x0 -> x5, waiting for transfers between devices: none -> 3580 us  [layer_full(): return latent_state + jnp.sum(lax.all_gather(update, 'blk'), axis=0)]
    psum x5 -> x0, waiting for transfers between devices: 1470 us -> none  [layer_full(): return latent_state + lax.psum(update, 'blk')]
    ppermute x4, starting transfers between devices: 113 us -> 21 us  [shifted(): lax.ppermute(value, axis, [(source, source + steps) for source in range(f...]
    reduce_sum x0 -> x5, other arithmetic: none -> 59.5 us  [layer_full(): return latent_state + jnp.sum(lax.all_gather(update, 'blk'), axis=0)]
where the time goes in v1:
time: 4530 us
  waiting for transfers between devices  4130 us (91%)
  blocking collectives  248 us (5%)
  other arithmetic  70.1 us (2%)
    all_gather x5, waiting for transfers between devices, layer_full(): return latent_state + jnp.sum(lax.all_gather(update, 'blk'), axis=0)  3580 us
    unnamed x12, waiting for transfers between devices  191 us
    unnamed x1, blocking collectives  131 us
    all_gather x1, waiting for transfers between devices, on_device(): tower_in = lax.all_gather(start_state, 'blk', axis=1, tiled=True)  129 us
    all_gather x1, waiting for transfers between devices, on_device(): gathered = lax.all_gather(latent_queries, 'blk', axis=1, tiled=True)  128 us
  transfers between devices with their start and end apart: 19, of which 19 were waited for; matrix products, arithmetic and copies ran while one was open for 0% of the time, Pallas kernels for 0%

profile of v1, /device:TPU:1, one launch (start us, length us, event | category | flops | bytes accessed | tf_op | source)
XLA Modules:
  0.0 4528.3 jit_solution(7864596417860312578)
XLA Ops:
  12.3 127.7 %all-gather.13.cloned.1.call-done = bf16[2,128,2048]{2,0,1:T(2,128)(2,1)} async-done(((bf16[2,4,2048]{2,0,1:T(2,128)(2,1)}), bf16[2,128,2048]{2,0,1:T(2,128)(2,1)}) %all-gather.13.cloned.1.call-update) | async-done | bytes 1048592 | tf_op jit(solution)/shard_map/all_gather | solution.py:67
  145.7 87.3 %pmax.7 = f32[2,16,128]{2,1,0:T(8,128)S(1)} all-reduce(f32[2,16,128]{2,1,0:T(8,128)S(1)} %get-tuple-element.11), channel_id=1, replica_groups=mesh['blk'=32,'segment'=4] {'blk','segment'}, use_global_device_ids=true, to_apply=%region_1.2 | all-reduce | flops 4096 | bytes 32768 | tf_op jit(solution)/shard_map/pmax | solution.py:79
  243.4 130.8 %all-reduce.1 = f32[2,128,16]{2,1,0:T(8,128)S(1)} all-reduce(f32[2,128,16]{2,1,0:T(8,128)S(1)} %copy.32), channel_id=8, replica_groups=mesh['blk'=32,'segment'=4] {'blk'}, use_global_device_ids=true, to_apply=%region_5.6.clone | all-reduce | flops 4096 | bytes 32768
  374.2 154.1 %all-reduce.7.cloned.1.call-done = f32[2,128,2048]{2,1,0:T(8,128)} async-done(((f32[2,128,2048]{2,1,0:T(8,128)}), f32[2,128,2048]{2,1,0:T(8,128)}) %all-reduce.7.cloned.1.call-update) | async-done | bytes 2097168
  530.0 29.5 psum.15
  559.6 34.4 all-reduce.5.cloned.1.call-done
  595.6 128.9 %all-gather.15.cloned.1.call-done = f32[2,128,2048]{2,0,1:T(2,128)} async-done(((f32[2,4,2048]{2,0,1:T(2,128)}), f32[2,128,2048]{2,0,1:T(2,128)}) %all-gather.15.cloned.1.call-update) | async-done | bytes 2097168 | tf_op jit(solution)/shard_map/all_gather | solution.py:102
  724.6 5.4 fusion.100
  736.4 731.7 %all-gather.17.cloned.1.call-done = f32[4096,2048]{1,0:T(8,128)} async-done(((f32[128,2048]{1,0:T(8,128)}), f32[4096,2048]{1,0:T(8,128)}) %all-gather.17.cloned.1.call-update) | async-done | bytes 33554448 | tf_op jit(solution)/shard_map/all_gather | solution.py:54
  1468.1 11.7 reduce_sum.147
  1480.4 5.4 collective-permute-start.1
  1485.8 12.2 collective-permute-done.1
  1505.4 712.9 %all-gather.19.cloned.1.call-done = f32[4096,2048]{1,0:T(8,128)} async-done(((f32[128,2048]{1,0:T(8,128)}), f32[4096,2048]{1,0:T(8,128)}) %all-gather.19.cloned.1.call-update) | async-done | bytes 33554448 | tf_op jit(solution)/shard_map/all_gather | solution.py:54
  2218.3 11.7 reduce_sum.150
  2235.3 12.4 collective-permute-done.3
  2253.4 712.9 %all-gather.21.cloned.1.call-done = f32[4096,2048]{1,0:T(8,128)} async-done(((f32[128,2048]{1,0:T(8,128)}), f32[4096,2048]{1,0:T(8,128)}) %all-gather.21.cloned.1.call-update) | async-done | bytes 33554448 | tf_op jit(solution)/shard_map/all_gather | solution.py:54
  2966.3 11.7 reduce_sum.153
  2983.3 12.4 collective-permute-done.5
  3001.4 712.9 %all-gather.23.cloned.1.call-done = f32[4096,2048]{1,0:T(8,128)} async-done(((f32[128,2048]{1,0:T(8,128)}), f32[4096,2048]{1,0:T(8,128)}) %all-gather.23.cloned.1.call-update) | async-done | bytes 33554448 | tf_op jit(solution)/shard_map/all_gather | solution.py:54
  3714.3 11.7 reduce_sum.156
  3732.3 12.4 collective-permute-done.7
  3750.4 712.9 %all-gather.25.cloned.1.call-done = f32[4096,2048]{1,0:T(8,128)} async-done(((f32[128,2048]{1,0:T(8,128)}), f32[4096,2048]{1,0:T(8,128)}) %all-gather.25.cloned.1.call-update) | async-done | bytes 33554448 | tf_op jit(solution)/shard_map/all_gather | solution.py:54
  4463.3 12.7 reduce_sum.159
  4483.1 36.3 reduce-scatter.6.cloned.1.call-done
  (113 shorter events, 81.7 us)
Async XLA Ops:
  6.5 135.9 %copy-start = (bf16[2,256,2048]{2,1,0:T(8,128)(2,1)S(1)}, bf16[2,256,2048]{2,1,0:T(8,128)(2,1)}, u32[]{:S(2)}) copy-start(bf16[2,256,2048]{2,1,0:T(8,128)(2,1)} %param.10) | copy-start | bytes 6291460
  6.5 133.4 %all-gather.13.cloned.1.call-start = ((), (), s32[]{:S(2)}) async-start(), calls=%async_computation.1 | async-start | bytes 1081344 | tf_op jit(solution)/shard_map/all_gather | solution.py:67
  8.1 520.2 %all-reduce.7.cloned.1.call-start = ((), (), s32[]{:S(2)}) async-start(), calls=%async_computation.10 | async-start | bytes 4194304
  238.9 355.1 %copy-start.6 = (bf16[2,4,2048]{2,1,0:T(4,128)(2,1)S(1)}, bf16[2,4,2048]{2,1,0:T(4,128)(2,1)}, u32[]{:S(2)}) copy-start(bf16[2,4,2048]{2,1,0:T(4,128)(2,1)} %param.9) | copy-start | bytes 98308
  238.9 355.1 %all-reduce.5.cloned.1.call-start = ((), (), s32[]{:S(2)}) async-start(), calls=%async_computation.2 | async-start | bytes 131072 | tf_op jit(solution)/shard_map/psum | solution.py:93
  243.3 487.0 %copy-start.2 = (bf16[1,2048,3,64]{1,3,2,0:T(8,128)(2,1)S(1)}, bf16[1,2048,3,64]{1,3,2,0:T(8,128)(2,1)}, u32[]{:S(2)}) copy-start(bf16[1,2048,3,64]{1,3,2,0:T(8,128)(2,1)} %param.14) | copy-start | bytes 2359300
  243.3 487.0 %copy-start.5 = (f32[1,2048]{1,0:T(1,128)S(1)}, f32[1,2048]{1,0:T(1,128)}, u32[]{:S(2)}) copy-start(f32[1,2048]{1,0:T(1,128)} %param.13) | copy-start | bytes 24580
  529.9 205.0 %copy-start.3 = (bf16[1,64,2048]{2,1,0:T(8,128)(2,1)S(1)}, bf16[1,64,2048]{2,1,0:T(8,128)(2,1)}, u32[]{:S(2)}) copy-start(bf16[1,64,2048]{2,1,0:T(8,128)(2,1)} %param.15) | copy-start | bytes 786436
  529.9 194.7 %all-gather.15.cloned.1.call-start = ((), (), s32[]{:S(2)}) async-start(), calls=%async_computation.3 | async-start | bytes 2162688 | tf_op jit(solution)/shard_map/all_gather | solution.py:102
  595.6 872.6 %all-gather.17.cloned.1.call-start = ((), (), s32[]{:S(2)}) async-start(), calls=%async_computation.4 | async-start | bytes 34603008 | tf_op jit(solution)/shard_map/all_gather | solution.py:54
  731.2 3.6 collective-permute-start
  736.4 1481.9 %all-gather.19.cloned.1.call-start = ((), (), s32[]{:S(2)}) async-start(), calls=%async_computation.5 | async-start | bytes 34603008 | tf_op jit(solution)/shard_map/all_gather | solution.py:54
  1480.4 17.6 collective-permute-start.1
  1500.6 3.2 collective-permute-start.2
  1505.3 1461.0 %all-gather.21.cloned.1.call-start = ((), (), s32[]{:S(2)}) async-start(), calls=%async_computation.6 | async-start | bytes 34603008 | tf_op jit(solution)/shard_map/all_gather | solution.py:54
  2230.1 17.6 collective-permute-start.3
  2248.6 3.2 collective-permute-start.4
  2253.3 1460.9 %all-gather.23.cloned.1.call-start = ((), (), s32[]{:S(2)}) async-start(), calls=%async_computation.7 | async-start | bytes 34603008 | tf_op jit(solution)/shard_map/all_gather | solution.py:54
  2978.1 17.6 collective-permute-start.5
  2996.6 3.2 collective-permute-start.6
  3001.3 1462.0 %all-gather.25.cloned.1.call-start = ((), (), s32[]{:S(2)}) async-start(), calls=%async_computation.8 | async-start | bytes 34603008 | tf_op jit(solution)/shard_map/all_gather | solution.py:54
  3727.1 17.6 collective-permute-start.7
  3745.6 3.2 collective-permute-start.8
  3750.4 769.1 %reduce-scatter.6.cloned.1.call-start = ((), (), s32[]{:S(2)}) async-start(), calls=%async_computation.9 | async-start | bytes 1310720
  (4 other events, 65.7 us)
Sparse Core Ops, SparseCore 0:
  9.0 130.9 all-gather.12
  239.0 289.2 all-reduce.6
  530.8 63.1 all-reduce.4
  595.7 128.8 all-gather.14
  736.5 731.6 all-gather.16
  1505.4 712.7 all-gather.18
  2253.4 712.7 all-gather.20
  3001.5 712.7 all-gather.22
  3750.5 712.7 all-gather.24
  4483.3 36.1 reduce-scatter.5
